TPU v7x, 32 devices: a whole 2x2x4 slice. The times are simulated.
32 devices in a mesh: seq: 4 (over y, core), head: 8 (over z, x).
Axes of the slice: x: 2, y: 2, z: 4, core: 2. Of those that a mesh axis runs over, the one named last changes fastest.
Arguments:
- inputs: bfloat16 [4096, 3, 2048], P(('seq', 'head')), may hold values from -6 to 6
- attn_gain: float32 [2048], replicated, may hold values from 0.25 to 1.75
- w_query: bfloat16 [2048, 256], P(None, 'head'), may hold values from -0.125 to 0.125
- w_key: bfloat16 [2048, 256], P(None, 'head'), may hold values from -0.125 to 0.125
- w_value: bfloat16 [2048, 2048], P(None, 'head'), may hold values from -0.125 to 0.125
- w_out: bfloat16 [2048, 2048], P('head'), may hold values from -1.5 to 1.5
- out_bias: float32 [2048], replicated, may hold values from -1.5 to 1.5
- mlp_gain: float32 [2048], replicated, may hold values from 0.25 to 1.75
- gate_weight: bfloat16 [2048, 5504], P(None, 'head'), may hold values from -0.125 to 0.125
- up_weight: bfloat16 [2048, 5504], P(None, 'head'), may hold values from -0.125 to 0.125
- down_weight: bfloat16 [5504, 2048], P('head'), may hold values from -0.078125 to 0.078125
- cotangent: bfloat16 [4096, 3, 2048], P(('seq', 'head')), may hold values from -6 to 6
- doc_lengths: int32 [3, 8], replicated, may hold values from 1 to 1536, 4096 in all within a row
Outputs:
- output: bfloat16 [4096, 3, 2048], P(('seq', 'head'))
- input_grad: bfloat16 [4096, 3, 2048], P(('seq', 'head'))
- attn_gain_grad: float32 [2048], P(('seq', 'head'))
- w_query_grad: float32 [2048, 256], P('seq', 'head')
- w_key_grad: float32 [2048, 256], P('seq', 'head')
- w_value_grad: float32 [2048, 2048], P('seq', 'head')
- w_out_grad: float32 [2048, 2048], P('head', 'seq')
- out_bias_grad: float32 [2048], P(('seq', 'head'))
- mlp_gain_grad: float32 [2048], P(('seq', 'head'))
- w_gate_grad: float32 [2048, 5504], P('seq', 'head')
- w_up_grad: float32 [2048, 5504], P('seq', 'head')
- w_down_grad: float32 [5504, 2048], P('head', 'seq')
Inputs may be any that keep to these rules, and one draw needn't show every extreme that they name: `doc_lengths`: in each row the 8 lengths sum to 4096 and the longest is exactly 1536.
All inputs are finite; a program needn't handle non-finite values.
Results may differ from a plain program's by a relative error of at most 0.02.
Values may be sent and summed in bfloat16 or wider, within the bound.
A program may use at most 320 MiB of HBM per device.

v0:
```python
import jax
import jax.numpy as jnp
from jax import lax
from jax.sharding import PartitionSpec as P

FEAT = 16
epsilon = 1e-05
root_half = 0.7071067811865476
exact_precision_flag = lax.Precision.HIGHEST


def entering(array, axis, join, neutral, backward):
    count = lax.axis_size(axis)
    place = lax.axis_index(axis)
    ahead = count - 1 - place if backward else place
    gathered = jax.tree.map(
        lambda a, kind: lax.all_gather(a.astype(kind), axis),
        array,
        (jnp.bfloat16, jnp.bfloat16, jnp.bfloat16),
    )
    state = jax.tree.map(lambda a, e: jnp.zeros_like(a) + jnp.asarray(e, a.dtype), array, neutral)

    def one(step, state):
        source = count - 1 - step if backward else step
        return join(
            state,
            jax.tree.map(
                lambda a, own: lax.dynamic_index_in_dim(a, source, 0, False).astype(own.dtype),
                gathered,
                array,
            ),
        )

    return lax.fori_loop(0, ahead, one, state)


def features(inputs):
    halved = inputs * 0.5
    size_in = inputs.shape[-1]
    squares = (halved[..., :, None] * halved[..., None, :]).reshape(
        inputs.shape[:-1] + (size_in * size_in,)
    ) * root_half
    return jnp.concatenate(
        [jnp.ones(inputs.shape[:-1] + (1,), inputs.dtype), halved, squares], axis=-1
    )


def doc_layout(doc_lengths, group_begin, group_len):
    doc_ends = jnp.cumsum(doc_lengths, axis=-1)
    positions = group_begin + jnp.arange(group_len, dtype=jnp.int32)
    passed = (doc_ends[..., :, None] <= positions).astype(jnp.int32)
    doc_index = jnp.sum(passed, axis=-2)
    doc_begin = jnp.sum(passed * doc_lengths[..., :, None], axis=-2)
    return (doc_index, doc_begin)


def chain_join(earlier, later):
    keep_prev = 1.0 - later[2]
    return (
        later[0] + keep_prev[:, None, None, None] * earlier[0],
        later[1] + keep_prev[:, None, None] * earlier[1],
        jnp.maximum(earlier[2], later[2]),
    )


def rms_scale(values_in):
    return lax.rsqrt(jnp.mean(values_in * values_in, axis=-1, keepdims=True) + epsilon)


def on_device(
    inputs,
    attn_gain,
    w_query,
    w_key,
    w_value,
    w_out,
    out_bias,
    mlp_gain,
    gate_weight,
    up_weight,
    down_weight,
    cotangent,
    doc_lengths,
):
    shard_len = inputs.shape[0]
    batch_rows = inputs.shape[1]
    head_local = w_query.shape[1] // FEAT
    value_dim = w_value.shape[1] // head_local
    group_len = shard_len * lax.axis_size("head")
    group_begin = lax.axis_index("seq") * group_len
    x_float = inputs.astype(jnp.float32)
    scale_one = rms_scale(x_float)
    normed_one = x_float * scale_one
    normed_low = (normed_one * attn_gain).astype(jnp.bfloat16)
    normed_full = lax.all_gather(normed_low, "head", axis=0, tiled=True)
    query_low = (
        jnp.einsum("trd,dc->trc", normed_full, w_query, preferred_element_type=jnp.float32)
        .astype(jnp.bfloat16)
        .reshape(group_len, batch_rows, head_local, FEAT)
    )
    key_low = (
        jnp.einsum("trd,dc->trc", normed_full, w_key, preferred_element_type=jnp.float32)
        .astype(jnp.bfloat16)
        .reshape(group_len, batch_rows, head_local, FEAT)
    )
    value_low = (
        jnp.einsum("trd,dc->trc", normed_full, w_value, preferred_element_type=jnp.float32)
        .astype(jnp.bfloat16)
        .reshape(group_len, batch_rows, head_local, value_dim)
    )
    doc_index, doc_begin = doc_layout(doc_lengths, group_begin, group_len)
    carried = (doc_begin < group_begin).astype(jnp.float32).T
    trailing = (doc_index == doc_index[:, -1:]).astype(jnp.float32).T
    restart = (doc_begin[:, -1] >= group_begin).astype(jnp.float32)
    positions = jnp.arange(group_len, dtype=jnp.int32)
    visible = (
        (positions[None, :] <= positions[:, None])[None]
        & (doc_index[:, :, None] == doc_index[:, None, :])
    )[:, None]
    scores = (
        jnp.einsum("trhf,urhf->rhtu", query_low, key_low, preferred_element_type=jnp.float32) * 0.25
    )
    weights_low = jnp.where(visible, 1.0 + scores + 0.5 * scores * scores, 0.0).astype(jnp.bfloat16)
    query_float = query_low.astype(jnp.float32)
    key_float = key_low.astype(jnp.float32)
    query_feat = features(query_float).astype(jnp.bfloat16)
    key_feat = features(key_float).astype(jnp.bfloat16)
    trail_low = trailing.astype(jnp.bfloat16)[:, :, None, None]
    local_state = jnp.einsum(
        "trhf,trhv->rhfv", key_feat, value_low * trail_low, preferred_element_type=jnp.float32
    )
    local_sum = jnp.sum(key_feat.astype(jnp.float32) * trailing[:, :, None, None], axis=0)
    empty_chain = (jnp.zeros_like(local_state), jnp.zeros_like(local_sum), jnp.zeros_like(restart))
    state_in, sum_in, _ = entering(
        (local_state, local_sum, restart), "seq", chain_join, empty_chain, False
    )
    state_low = state_in.astype(jnp.bfloat16)
    numerator = jnp.einsum(
        "rhtu,urhv->trhv", weights_low, value_low, preferred_element_type=jnp.float32
    )
    numerator = numerator + carried[:, :, None, None] * jnp.einsum(
        "trhf,rhfv->trhv", query_feat, state_low, preferred_element_type=jnp.float32
    )
    query_feat_float = query_feat.astype(jnp.float32)
    denominator = jnp.transpose(jnp.sum(weights_low, axis=-1, dtype=jnp.float32), (2, 0, 1))
    denominator = denominator + carried[:, :, None] * jnp.einsum(
        "trhf,rhf->trh", query_feat_float, sum_in, precision=exact_precision_flag
    )
    attended = (
        (numerator / denominator[..., None])
        .astype(jnp.bfloat16)
        .reshape(group_len, batch_rows, head_local * value_dim)
    )
    row_segment = attended
    attn_branch = lax.psum_scatter(
        jnp.einsum("trc,cd->trd", row_segment, w_out, preferred_element_type=jnp.float32),
        "head",
        scatter_dimension=0,
        tiled=True,
    )
    middle = x_float + attn_branch + out_bias
    scale_two = rms_scale(middle)
    second_normed = middle * scale_two
    normed_two_low = (second_normed * mlp_gain).astype(jnp.bfloat16)

    def projections(row_segment):
        gate_segment = jnp.einsum(
            "czm,my->czy", row_segment, gate_weight, preferred_element_type=jnp.float32
        )
        up_segment = jnp.einsum(
            "czm,my->czy", row_segment, up_weight, preferred_element_type=jnp.float32
        )
        return (gate_segment, up_segment)

    gate_segment, up_segment = projections(
        lax.all_gather(normed_two_low, "head", axis=0, tiled=True)
    )
    hidden_activation = (jax.nn.silu(gate_segment) * up_segment).astype(jnp.bfloat16)
    row_segment = hidden_activation
    perceptron_branch = lax.psum_scatter(
        jnp.einsum(
            "nzh,hi->nzi", row_segment, down_weight, preferred_element_type=jnp.float32
        ).astype(jnp.bfloat16),
        "head",
        scatter_dimension=0,
        tiled=True,
    ).astype(jnp.float32)
    output = (middle + perceptron_branch).astype(jnp.bfloat16)
    second_normed_complete, gradient_complete = (
        lax.all_gather(normed_two_low, "head", axis=0, tiled=True),
        lax.all_gather(cotangent, "head", axis=0, tiled=True),
    )
    gate_projected, up_projected = projections(second_normed_complete)
    down_weight_gradient = jnp.einsum(
        "ebn,eby->ny", hidden_activation, gradient_complete, preferred_element_type=jnp.float32
    )
    hidden_gradient = jnp.einsum(
        "bje,ke->bjk", gradient_complete, down_weight, preferred_element_type=jnp.float32
    )
    sigmoid_gate = jax.nn.sigmoid(gate_projected)
    gate_gradient = (
        hidden_gradient
        * up_projected
        * sigmoid_gate
        * (1.0 + gate_projected * (1.0 - sigmoid_gate))
    ).astype(jnp.bfloat16)
    up_gradient = (hidden_gradient * gate_projected * sigmoid_gate).astype(jnp.bfloat16)
    grad_w_gate = jnp.einsum(
        "ego,egv->ov", second_normed_complete, gate_gradient, preferred_element_type=jnp.float32
    )
    grad_w_up = jnp.einsum(
        "ego,egv->ov", second_normed_complete, up_gradient, preferred_element_type=jnp.float32
    )
    grad_normed_two = lax.psum_scatter(
        (
            jnp.einsum(
                "szq,hq->szh", gate_gradient, gate_weight, preferred_element_type=jnp.float32
            )
            + jnp.einsum("szq,hq->szh", up_gradient, up_weight, preferred_element_type=jnp.float32)
        ).astype(jnp.bfloat16),
        "head",
        scatter_dimension=0,
        tiled=True,
    ).astype(jnp.float32)
    gain_two_part = jnp.sum(grad_normed_two * second_normed, axis=(0, 1))
    grad_scaled_two = grad_normed_two * mlp_gain
    grad_middle = cotangent.astype(jnp.float32) + scale_two * (
        grad_scaled_two
        - second_normed * jnp.mean(grad_scaled_two * second_normed, axis=-1, keepdims=True)
    )
    bias_part = jnp.sum(grad_middle, axis=(0, 1))
    grad_branch = lax.all_gather(grad_middle.astype(jnp.bfloat16), "head", axis=0, tiled=True)
    grad_w_out = jnp.einsum(
        "trc,trd->cd", attended, grad_branch, preferred_element_type=jnp.float32
    )
    grad_attended = jnp.einsum(
        "trd,cd->trc", grad_branch, w_out, preferred_element_type=jnp.float32
    ).reshape(group_len, batch_rows, head_local, value_dim)
    grad_numer = (grad_attended / denominator[..., None]).astype(jnp.bfloat16)
    grad_denom = -jnp.sum(grad_attended * numerator, axis=-1) / (denominator * denominator)
    grad_weights = (
        jnp.einsum("trhv,urhv->rhtu", grad_numer, value_low, preferred_element_type=jnp.float32)
        + jnp.transpose(grad_denom, (1, 2, 0))[..., None]
    )
    grad_scores = jnp.where(visible, grad_weights * (1.0 + scores), 0.0).astype(jnp.bfloat16)
    grad_query = (
        jnp.einsum("rhtu,urhf->trhf", grad_scores, key_low, preferred_element_type=jnp.float32)
        * 0.25
    )
    grad_key = (
        jnp.einsum("rhtu,trhf->urhf", grad_scores, query_low, preferred_element_type=jnp.float32)
        * 0.25
    )
    grad_value = jnp.einsum(
        "rhtu,trhv->urhv", weights_low, grad_numer, preferred_element_type=jnp.float32
    )
    carry_low = carried.astype(jnp.bfloat16)[:, :, None, None]
    grad_state_in = jnp.einsum(
        "trhf,trhv->rhfv", query_feat, grad_numer * carry_low, preferred_element_type=jnp.float32
    )
    grad_sum_in = jnp.einsum(
        "trhf,trh->rhf",
        query_feat_float,
        carried[:, :, None] * grad_denom,
        precision=exact_precision_flag,
    )
    grad_query_feat = carried[:, :, None, None] * (
        jnp.einsum("trhv,rhfv->trhf", grad_numer, state_low, preferred_element_type=jnp.float32)
        + grad_denom[..., None] * sum_in[None]
    )
    empty_grads = (
        jnp.zeros_like(grad_state_in),
        jnp.zeros_like(grad_sum_in),
        jnp.zeros_like(restart),
    )
    grad_state_out, grad_sum_out, _ = entering(
        (grad_state_in, grad_sum_in, restart), "seq", chain_join, empty_grads, True
    )
    grad_state_low = grad_state_out.astype(jnp.bfloat16)
    grad_key_feat = trailing[:, :, None, None] * (
        jnp.einsum("trhv,rhfv->trhf", value_low, grad_state_low, preferred_element_type=jnp.float32)
        + grad_sum_out[None]
    )
    grad_value = grad_value + trailing[:, :, None, None] * jnp.einsum(
        "trhf,rhfv->trhv", key_feat, grad_state_low, preferred_element_type=jnp.float32
    )
    _, query_map_back = jax.vjp(features, query_float)
    _, key_map_back = jax.vjp(features, key_float)
    grad_query = grad_query + query_map_back(grad_query_feat)[0]
    grad_key = grad_key + key_map_back(grad_key_feat)[0]
    grad_query_low = grad_query.astype(jnp.bfloat16).reshape(
        group_len, batch_rows, head_local * FEAT
    )
    grad_key_low = grad_key.astype(jnp.bfloat16).reshape(group_len, batch_rows, head_local * FEAT)
    grad_value_low = grad_value.astype(jnp.bfloat16).reshape(
        group_len, batch_rows, head_local * value_dim
    )
    grad_w_query = jnp.einsum(
        "trd,trc->dc", normed_full, grad_query_low, preferred_element_type=jnp.float32
    )
    grad_w_key = jnp.einsum(
        "trd,trc->dc", normed_full, grad_key_low, preferred_element_type=jnp.float32
    )
    grad_w_value = jnp.einsum(
        "trd,trc->dc", normed_full, grad_value_low, preferred_element_type=jnp.float32
    )
    summed = jnp.einsum("trc,dc->trd", grad_query_low, w_query, preferred_element_type=jnp.float32)
    summed = summed + jnp.einsum(
        "trc,dc->trd", grad_key_low, w_key, preferred_element_type=jnp.float32
    )
    grad_normed_one = lax.psum_scatter(
        (
            summed
            + jnp.einsum("trc,dc->trd", grad_value_low, w_value, preferred_element_type=jnp.float32)
        ).astype(jnp.bfloat16),
        "head",
        scatter_dimension=0,
        tiled=True,
    ).astype(jnp.float32)
    gain_one_part = jnp.sum(grad_normed_one * normed_one, axis=(0, 1))
    grad_scaled_one = grad_normed_one * attn_gain
    input_grad = (
        grad_middle
        + scale_one
        * (
            grad_scaled_one
            - normed_one * jnp.mean(grad_scaled_one * normed_one, axis=-1, keepdims=True)
        )
    ).astype(jnp.bfloat16)
    gain_one, bias_grad, gain_two = (
        lax.psum_scatter(gain_one_part, ("seq", "head"), scatter_dimension=0, tiled=True),
        lax.psum_scatter(bias_part, ("seq", "head"), scatter_dimension=0, tiled=True),
        lax.psum_scatter(gain_two_part, ("seq", "head"), scatter_dimension=0, tiled=True),
    )
    summed_query, summed_key, summed_value, summed_out, summed_gate, summed_up, summed_down = (
        lax.psum_scatter(
            grad_w_query.astype(jnp.bfloat16), "seq", scatter_dimension=0, tiled=True
        ).astype(jnp.float32),
        lax.psum_scatter(
            grad_w_key.astype(jnp.bfloat16), "seq", scatter_dimension=0, tiled=True
        ).astype(jnp.float32),
        lax.psum_scatter(
            grad_w_value.astype(jnp.bfloat16), "seq", scatter_dimension=0, tiled=True
        ).astype(jnp.float32),
        lax.psum_scatter(
            grad_w_out.astype(jnp.bfloat16), "seq", scatter_dimension=1, tiled=True
        ).astype(jnp.float32),
        lax.psum_scatter(
            grad_w_gate.astype(jnp.bfloat16), "seq", scatter_dimension=0, tiled=True
        ).astype(jnp.float32),
        lax.psum_scatter(
            grad_w_up.astype(jnp.bfloat16), "seq", scatter_dimension=0, tiled=True
        ).astype(jnp.float32),
        lax.psum_scatter(
            down_weight_gradient.astype(jnp.bfloat16), "seq", scatter_dimension=1, tiled=True
        ).astype(jnp.float32),
    )
    return (
        output,
        input_grad,
        gain_one,
        summed_query,
        summed_key,
        summed_value,
        summed_out,
        bias_grad,
        gain_two,
        summed_gate,
        summed_up,
        summed_down,
    )


def solution(mesh):
    placed = (
        P(("seq", "head"), None, None),
        P(),
        P(None, "head"),
        P(None, "head"),
        P(None, "head"),
        P("head", None),
        P(),
        P(),
        P(None, "head"),
        P(None, "head"),
        P("head", None),
        P(("seq", "head"), None, None),
        P(),
    )
    return jax.shard_map(
        on_device,
        mesh=mesh,
        in_specs=placed,
        out_specs=(
            P(("seq", "head"), None, None),
            P(("seq", "head"), None, None),
            P(("seq", "head")),
            P("seq", "head"),
            P("seq", "head"),
            P("seq", "head"),
            P("head", "seq"),
            P(("seq", "head")),
            P(("seq", "head")),
            P("seq", "head"),
            P("seq", "head"),
            P("head", "seq"),
        ),
        check_vma=False,
    )
```

profile of v0, /device:TPU:0, one launch (start us, length us, event | category | flops | bytes accessed | tf_op | source)
XLA Modules:
  0.0 2234.3 jit_solution(17653696838373602096)
XLA Ops:
  14.8 8.3 all-reduce
  28.0 164.0 %all-gather.12.cloned.1.call-done = bf16[1024,3,2048]{2,0,1:T(8,128)(2,1)} async-done(((bf16[128,3,2048]{2,0,1:T(8,128)(2,1)}), bf16[1024,3,2048]{2,0,1:T(8,128)(2,1)}) %all-gather.12.cloned.1.call-update) | async-done | bytes 12582928 | tf_op jit(solution)/shard_map/all_gather | solution.py:95
  192.1 8.6 convolution_convert_fusion.3
  206.8 14.2 convolution_convert_fusion.1
  224.8 4.0 fusion.47
  230.0 3.9 multiply_reduce_fusion
  233.9 5.2 all-gather.2
  241.7 15.4 convert_reduce_fusion
  257.1 8.1 fusion.97
  267.1 4.5 fusion.90
  271.6 4.6 divide_convert_fusion.1
  277.5 10.1 fusion.61
  287.7 412.3 %reduce-scatter.12.cloned.1.call-done = f32[128,3,2048]{2,0,1:T(8,128)} async-done(((f32[1024,3,2048]{2,0,1:T(8,128)}), f32[128,3,2048]{2,0,1:T(8,128)}) %reduce-scatter.12.cloned.1.call-update) | async-done | bytes 3145744 | tf_op jit(solution)/shard_map/reduce_scatter | solution.py:155
  707.0 174.9 %all-gather.14.cloned.1.call-done = bf16[1024,3,2048]{2,0,1:T(8,128)(2,1)} async-done(((bf16[128,3,2048]{2,0,1:T(8,128)(2,1)}), bf16[1024,3,2048]{2,0,1:T(8,128)(2,1)}) %all-gather.14.cloned.1.call-update) | async-done | bytes 12582928 | tf_op jit(solution)/shard_map/all_gather | solution.py:176
  881.9 15.0 fusion.33
  896.8 11.2 fusion.37
  908.1 150.5 %all-gather.16.cloned.1.call-done = bf16[1024,3,2048]{2,0,1:T(8,128)(2,1)} async-done(((bf16[128,3,2048]{2,0,1:T(8,128)(2,1)}), bf16[1024,3,2048]{2,0,1:T(8,128)(2,1)}) %all-gather.16.cloned.1.call-update) | async-done | bytes 12582928 | tf_op jit(solution)/shard_map/all_gather | solution.py:191
  1058.5 22.0 multiply_convert_fusion
  1080.6 17.3 fusion.35
  1097.9 18.9 add_convert_fusion.1
  1116.9 15.2 convolution_convert_fusion
  1132.2 190.8 %reduce-scatter.16.cloned.1.call-done = bf16[128,3,2048]{2,0,1:T(8,128)(2,1)} async-done(((bf16[1024,3,2048]{2,0,1:T(8,128)(2,1)}), bf16[128,3,2048]{2,0,1:T(8,128)(2,1)}) %reduce-scatter.16.cloned.1.call-update) | async-done | bytes 1572880 | tf_op jit(solution)/shard_map/reduce_scatter | solution.py:214
  1323.0 4.0 fusion.20
  1327.0 206.5 %reduce-scatter.14.cloned.1.call-done = bf16[128,3,2048]{2,0,1:T(8,128)(2,1)} async-done(((bf16[1024,3,2048]{2,0,1:T(8,128)(2,1)}), bf16[128,3,2048]{2,0,1:T(8,128)(2,1)}) %reduce-scatter.14.cloned.1.call-update) | async-done | bytes 1572880 | tf_op jit(solution)/shard_map/reduce_scatter | solution.py:180
  1533.4 6.0 fusion.93
  1542.5 175.6 %all-gather.18.cloned.1.call-done = bf16[1024,3,2048]{2,0,1:T(8,128)(2,1)} async-done(((bf16[128,3,2048]{2,0,1:T(8,128)(2,1)}), bf16[1024,3,2048]{2,0,1:T(8,128)(2,1)}) %all-gather.18.cloned.1.call-update) | async-done | bytes 12582928 | tf_op jit(solution)/shard_map/all_gather | solution.py:232
  1718.2 9.0 multiply_reduce_fusion.5
  1732.1 14.5 bitcast_convert_fusion
  1746.7 14.4 bitcast_convert_fusion.1
  1761.1 14.6 bitcast_convert_fusion.2
  1783.6 17.5 select_convert_fusion
  1801.1 6.5 fusion.57
  1810.6 10.3 fusion.78
  1820.9 10.6 fusion.98
  1831.7 9.9 fusion.40
  1841.6 4.9 fusion.88
  1846.5 5.2 all-gather.4
  1851.9 4.9 while.31
  1856.8 5.8 fusion.27
  1870.5 8.2 fusion.58
  1881.7 10.4 fusion.63
  1892.3 7.7 fusion.39
  1900.1 22.1 add_convert_fusion
  1932.7 5.6 reduce-scatter.22.cloned.1.call-done
  1939.7 26.5 %reduce-scatter.24.cloned.1.call-done = bf16[512,256]{1,0:T(8,128)(2,1)} async-done(((bf16[2048,256]{1,0:T(8,128)(2,1)}), bf16[512,256]{1,0:T(8,128)(2,1)}) %reduce-scatter.24.cloned.1.call-update) | async-done | bytes 262160 | tf_op jit(solution)/shard_map/reduce_scatter | solution.py:342
  1968.0 209.8 %reduce-scatter.18.cloned.1.call-done = bf16[128,3,2048]{2,0,1:T(8,128)(2,1)} async-done(((bf16[1024,3,2048]{2,0,1:T(8,128)(2,1)}), bf16[128,3,2048]{2,0,1:T(8,128)(2,1)}) %reduce-scatter.18.cloned.1.call-update) | async-done | bytes 1572880 | tf_op jit(solution)/shard_map/reduce_scatter | solution.py:311
  2181.0 39.7 %all-reduce.4 = (f32[2048]{0:T(1024)S(1)}, f32[2048]{0:T(1024)S(1)}, f32[2048]{0:T(1024)S(1)}) all-reduce(f32[2048]{0:T(1024)S(1)} %get-tuple-element.232, f32[2048]{0:T(1024)S(1)} %copy-done.57, f32[2048]{0:T(1024)S(1)} %copy-done.56), channel_id=11, replica_groups=mesh['seq'=4,'head'=8] {'seq','head'}, use_global_device_ids=true, to_apply=%region_23.24.clone | all-reduce | flops 6144 | bytes 49152
  2222.4 4.9 fusion.16
  (268 shorter events, 89.2 us)
Async XLA Ops:
  7.2 1051.4 %copy-start = (bf16[688,2048]{1,0:T(8,128)(2,1)S(1)}, bf16[688,2048]{1,0:T(8,128)(2,1)}, u32[]{:S(2)}) copy-start(bf16[688,2048]{1,0:T(8,128)(2,1)} %param.27) | copy-start | bytes 8454148
  7.2 184.8 %all-gather.12.cloned.1.call-start = ((), (), s32[]{:S(2)}) async-start(), calls=%async_computation.11 | async-start | bytes 14155776 | tf_op jit(solution)/shard_map/all_gather | solution.py:95
  12.7 179.3 %copy-start.38 = (bf16[2048,32]{0,1:T(8,128)(2,1)S(1)}, bf16[2048,32]{0,1:T(8,128)(2,1)}, u32[]{:S(2)}) copy-start(bf16[2048,32]{0,1:T(8,128)(2,1)} %param.19) | copy-start | bytes 393220
  12.8 252.4 %all-gather.20.cloned.1.call-start = ((), (), s32[]{:S(2)}) async-start(), calls=%async_computation.26 | async-start | bytes 2096640 | tf_op jit(solution)/shard_map/all_gather | solution.py:17
  23.3 248.3 %copy-start.63 = (bf16[273]{0:T(512)(128)(2,1)}, bf16[273]{0:T(512)(128)(2,1)S(1)}, u32[]{:S(2)}) copy-start(bf16[273]{0:T(512)(128)(2,1)S(1)} %pad.3.clone) | copy-start | bytes 1642
  24.4 247.2 %copy-start.35 = (f32[3,1024]{1,0:T(4,128)}, f32[3,1024]{1,0:T(4,128)S(1)}, u32[]{:S(2)}) copy-start(f32[3,1024]{1,0:T(4,128)S(1)} %get-tuple-element.276) | copy-start | bytes 36868
  24.5 205.6 %copy-start.44 = (f32[1024,3]{0,1:T(4,128)}, f32[1024,3]{0,1:T(4,128)S(1)}, u32[]{:S(2)}) copy-start(f32[1024,3]{0,1:T(4,128)S(1)} %get-tuple-element.282) | copy-start | bytes 36868
  28.0 173.5 %copy-start.40 = (bf16[2048,32]{0,1:T(8,128)(2,1)S(1)}, bf16[2048,32]{0,1:T(8,128)(2,1)}, u32[]{:S(2)}) copy-start(bf16[2048,32]{0,1:T(8,128)(2,1)} %param.20) | copy-start | bytes 393220
  200.6 41.1 %copy-start.25 = (bf16[1024,3,32]{0,2,1:T(8,128)(2,1)}, bf16[1024,3,32]{0,2,1:T(8,128)(2,1)S(1)}, u32[]{:S(2)}) copy-start(bf16[1024,3,32]{0,2,1:T(8,128)(2,1)S(1)} %convolution_convert_fusion.3) | copy-start | bytes 589828
  206.8 17.1 copy-start.16
  230.0 470.0 %reduce-scatter.12.cloned.1.call-start = ((), (), s32[]{:S(2)}) async-start(), calls=%async_computation.12 | async-start | bytes 28311552 | tf_op jit(solution)/shard_map/reduce_scatter | solution.py:155
  241.7 15.4 copy-start.9
  257.1 14.5 copy-start.50
  287.6 412.4 %copy-start.60 = (f32[2048]{0:T(1024)S(1)}, f32[2048]{0:T(1024)}, u32[]{:S(2)}) copy-start(f32[2048]{0:T(1024)} %param.23) | copy-start | bytes 24580
  287.6 417.1 %copy-start.54 = (f32[2048]{0:T(1024)S(1)}, f32[2048]{0:T(1024)}, u32[]{:S(2)}) copy-start(f32[2048]{0:T(1024)} %param.24) | copy-start | bytes 24580
  287.6 594.2 %all-gather.14.cloned.1.call-start = ((), (), s32[]{:S(2)}) async-start(), calls=%async_computation.13 | async-start | bytes 14155776 | tf_op jit(solution)/shard_map/all_gather | solution.py:176
  706.1 352.4 %all-gather.16.cloned.1.call-start = ((), (), s32[]{:S(2)}) async-start(), calls=%async_computation.15 | async-start | bytes 14155776 | tf_op jit(solution)/shard_map/all_gather | solution.py:191
  706.7 616.2 %reduce-scatter.16.cloned.1.call-start = ((), (), s32[]{:S(2)}) async-start(), calls=%async_computation.16 | async-start | bytes 14155776 | tf_op jit(solution)/shard_map/reduce_scatter | solution.py:214
  881.9 15.0 copy-start.65
  881.9 15.0 copy-start.66
  1116.8 416.6 %reduce-scatter.14.cloned.1.call-start = ((), (), s32[]{:S(2)}) async-start(), calls=%async_computation.14 | async-start | bytes 14155776 | tf_op jit(solution)/shard_map/reduce_scatter | solution.py:180
  1132.1 401.3 %copy-start.20 = (bf16[128,3,2048]{2,0,1:T(8,128)(2,1)S(1)}, bf16[128,3,2048]{2,0,1:T(8,128)(2,1)}, u32[]{:S(2)}) copy-start(bf16[128,3,2048]{2,0,1:T(8,128)(2,1)} %param.28) | copy-start | bytes 4718596
  1132.1 586.0 %all-gather.18.cloned.1.call-start = ((), (), s32[]{:S(2)}) async-start(), calls=%async_computation.17 | async-start | bytes 14155776 | tf_op jit(solution)/shard_map/all_gather | solution.py:232
  1539.4 178.7 %copy-start.32 = (bf16[256,2048]{1,0:T(8,128)(2,1)S(1)}, bf16[256,2048]{1,0:T(8,128)(2,1)}, u32[]{:S(2)}) copy-start(bf16[256,2048]{1,0:T(8,128)(2,1)} %param.22) | copy-start | bytes 3145732
  1542.5 309.3 %all-gather.22.cloned.1.call-start = ((), (), s32[]{:S(2)}) async-start(), calls=%async_computation.27 | async-start | bytes 2096640 | tf_op jit(solution)/shard_map/all_gather | solution.py:17
  1727.6 48.3 %copy-start.12 = (bf16[1024,3,2,128]{0,3,2,1:T(8,128)(2,1)}, bf16[1024,3,2,128]{0,3,2,1:T(8,128)(2,1)S(1)}, u32[]{:S(2)}) copy-start(bf16[1024,3,2,128]{0,3,2,1:T(8,128)(2,1)S(1)} %divide_convert_fusion) | copy-start | bytes 4718596
  1732.1 190.3 %reduce-scatter.32.cloned.1.call-start = ((), (), s32[]{:S(2)}) async-start(), calls=%async_computation.25 | async-start | bytes 3522560 | tf_op jit(solution)/shard_map/reduce_scatter | solution.py:354
  1746.6 178.1 %reduce-scatter.30.cloned.1.call-start = ((), (), s32[]{:S(2)}) async-start(), calls=%async_computation.24 | async-start | bytes 3522560 | tf_op jit(solution)/shard_map/reduce_scatter | solution.py:351
  1761.0 166.1 %reduce-scatter.28.cloned.1.call-start = ((), (), s32[]{:S(2)}) async-start(), calls=%async_computation.23 | async-start | bytes 3522560 | tf_op jit(solution)/shard_map/reduce_scatter | solution.py:348
  1761.1 14.8 copy-start.36
  1761.1 14.8 copy-start.51
  1761.1 14.8 copy-start.53
  1761.1 14.8 copy-start.7
  1761.1 14.8 copy-start.43
  1775.8 153.7 %reduce-scatter.20.cloned.1.call-start = ((), (), s32[]{:S(2)}) async-start(), calls=%async_computation.19 | async-start | bytes 163840 | tf_op jit(solution)/shard_map/reduce_scatter | solution.py:336
  1780.0 27.6 %slice-start = ((s8[12582912]{0:T(1024)(128)(4,1)}), s8[4194304]{0:T(1024)(128)(4,1)S(1)}, s32[]{:S(2)}) async-start(s8[12582912]{0:T(1024)(128)(4,1)} %bitcast.219), calls=%async_computation.28 | async-start | bytes 8388608
  1783.6 17.5 copy-start.28
  1783.6 24.0 %slice-start.1 = ((s8[12582912]{0:T(1024)(128)(4,1)}), s8[4194304]{0:T(1024)(128)(4,1)S(1)}, s32[]{:S(2)}) async-start(s8[12582912]{0:T(1024)(128)(4,1)} %bitcast.219), calls=%async_computation.29 | async-start | bytes 8388608
  1783.6 24.0 %slice-start.2 = ((s8[12582912]{0:T(1024)(128)(4,1)}), s8[4194304]{0:T(1024)(128)(4,1)S(1)}, s32[]{:S(2)}) async-start(s8[12582912]{0:T(1024)(128)(4,1)} %bitcast.219), calls=%async_computation.30 | async-start | bytes 8388608
  1831.5 99.5 %reduce-scatter.26.cloned.1.call-start = ((), (), s32[]{:S(2)}) async-start(), calls=%async_computation.22 | async-start | bytes 1310720 | tf_op jit(solution)/shard_map/reduce_scatter | solution.py:345
  1851.7 86.6 %reduce-scatter.22.cloned.1.call-start = ((), (), s32[]{:S(2)}) async-start(), calls=%async_computation.20 | async-start | bytes 163840 | tf_op jit(solution)/shard_map/reduce_scatter | solution.py:339
  1892.1 74.1 %reduce-scatter.24.cloned.1.call-start = ((), (), s32[]{:S(2)}) async-start(), calls=%async_computation.21 | async-start | bytes 1310720 | tf_op jit(solution)/shard_map/reduce_scatter | solution.py:342
  1900.1 277.7 %reduce-scatter.18.cloned.1.call-start = ((), (), s32[]{:S(2)}) async-start(), calls=%async_computation.18 | async-start | bytes 14155776 | tf_op jit(solution)/shard_map/reduce_scatter | solution.py:311
  1922.3 255.5 %copy-start.55 = (f32[2048]{0:T(1024)S(1)}, f32[2048]{0:T(1024)}, u32[]{:S(2)}) copy-start(f32[2048]{0:T(1024)} %param.18) | copy-start | bytes 24580
  1922.3 255.5 %copy-start.59 = (f32[128,3]{0,1:T(4,128)S(1)}, f32[128,3]{0,1:T(4,128)}, u32[]{:S(2)}) copy-start(f32[128,3]{0,1:T(4,128)} %copy-done.58) | copy-start | bytes 4612
  1924.7 256.2 %copy-start.56 = (f32[2048]{0:T(1024)S(1)}, f32[2048]{0:T(1024)}, u32[]{:S(2)}) copy-start(f32[2048]{0:T(1024)} %get-tuple-element.230) | copy-start | bytes 24580
  1924.7 256.2 %copy-start.57 = (f32[2048]{0:T(1024)S(1)}, f32[2048]{0:T(1024)}, u32[]{:S(2)}) copy-start(f32[2048]{0:T(1024)} %get-tuple-element.271) | copy-start | bytes 24580
  2177.8 49.5 %copy-start.1 = (bf16[688,2048]{1,0:T(8,128)(2,1)S(1)}, bf16[688,2048]{1,0:T(8,128)(2,1)}, u32[]{:S(2)}) copy-start(bf16[688,2048]{1,0:T(8,128)(2,1)} %param.27) | copy-start | bytes 8454148
  (45 other events, 235.8 us)
Sparse Core Ops, SparseCore 0:
  12.9 179.1 all-gather.11
  230.1 18.4 all-gather.19
  287.7 412.2 reduce-scatter.11
  706.3 175.5 all-gather.13
  883.9 174.6 all-gather.15
  1116.9 205.9 reduce-scatter.15
  1326.6 206.8 reduce-scatter.13
  1542.6 175.5 all-gather.17
  1732.2 18.4 all-gather.21
  1753.1 35.9 reduce-scatter.31
  1791.8 35.9 reduce-scatter.29
  1830.2 36.0 reduce-scatter.27
  1869.4 19.5 reduce-scatter.19
  1891.4 24.8 reduce-scatter.25
  1918.7 19.5 reduce-scatter.21
  1941.3 24.8 reduce-scatter.23
  1970.1 207.6 reduce-scatter.17
where the time goes:
time: 2240 us; the launch traced here: 2230 us
  waiting for transfers between devices  1720 us (77%)
  matrix products  349 us (16%)
  other arithmetic  66.9 us (3%)
  blocking collectives  58.4 us (3%)
  local copies, waits for them, and re-layouts  25.8 us (1%)
    reduce_scatter x1, waiting for transfers between devices, on_device(): lax.psum_scatter(jnp.einsum('trc,cd->trd', row_segment, w_out, preferred_...  412 us
    reduce_scatter x1, waiting for transfers between devices, on_device(): lax.psum_scatter((summed + jnp.einsum('trc,dc->trd', grad_value_low, w_va...  210 us
    reduce_scatter x1, waiting for transfers between devices, on_device(): lax.psum_scatter(jnp.einsum('nzh,hi->nzi', row_segment, down_weight, pref...  206 us
    reduce_scatter x1, waiting for transfers between devices, on_device(): lax.psum_scatter((jnp.einsum('szq,hq->szh', gate_gradient, gate_weight, p...  191 us
    all_gather x1, waiting for transfers between devices, on_device(): lax.all_gather(grad_middle.astype(jnp.bfloat16), 'head', axis=0, tiled=True)  176 us
    all_gather x1, waiting for transfers between devices, on_device(): lax.all_gather(normed_two_low, 'head', axis=0, tiled=True)  175 us
    all_gather x1, waiting for transfers between devices, on_device(): normed_full = lax.all_gather(normed_low, 'head', axis=0, tiled=True)  164 us
    all_gather x1, waiting for transfers between devices, on_device(): lax.all_gather(cotangent, 'head', axis=0, tiled=True)  150 us
  transfers between devices with their start and end apart: 17, of which 10 were waited for; matrix products, arithmetic and copies ran while one was open for 12% of the time, Pallas kernels for 0%

commit v1 on v0

--- a/solution.py
+++ b/solution.py
@@ -92,7 +92,12 @@
     scale_one = rms_scale(x_float)
     normed_one = x_float * scale_one
     normed_low = (normed_one * attn_gain).astype(jnp.bfloat16)
-    normed_full = lax.all_gather(normed_low, "head", axis=0, tiled=True)
+    ring = [normed_low]
+    for hop in range(7):
+        ring.append(lax.ppermute(ring[-1], "head", [(dev, (dev + 1) % 8) for dev in range(8)]))
+    normed_full = jnp.roll(
+        jnp.concatenate(ring[::-1], axis=0), (lax.axis_index("head") + 1) * ring[0].shape[0], axis=0
+    )
     query_low = (
         jnp.einsum("trd,dc->trc", normed_full, w_query, preferred_element_type=jnp.float32)
         .astype(jnp.bfloat16)

time: 2240 us -> 2330 us (1.040)
  waiting for transfers between devices: 1720 us -> 1790 us
    ppermute x0 -> x7, waiting for transfers between devices: none -> 241 us  [on_device(): lax.ppermute(ring[-1], 'head', [(dev, (dev + 1) % 8) for dev in range(8)])]
    all_gather x1 -> x0, waiting for transfers between devices: 164 us -> none  [on_device(): normed_full = lax.all_gather(normed_low, 'head', axis=0, tiled=True)]
  transfers between devices with their start and end apart: 17 -> 23, of which waited for: 10 -> 16; matrix products, arithmetic and copies ran while one was open for 12% -> 12% of each run, Pallas kernels for 0% -> 0%
where the time goes in v1:
time: 2330 us; the launch traced here: 2320 us
  waiting for transfers between devices  1790 us (77%)
  matrix products  352 us (15%)
  other arithmetic  67.7 us (3%)
  blocking collectives  55.9 us (2%)
  local copies, waits for them, and re-layouts  38.2 us (2%)
    reduce_scatter x1, waiting for transfers between devices, on_device(): lax.psum_scatter(jnp.einsum('trc,cd->trd', row_segment, w_out, preferred_...  410 us
    ppermute x7, waiting for transfers between devices, on_device(): lax.ppermute(ring[-1], 'head', [(dev, (dev + 1) % 8) for dev in range(8)])  241 us
    reduce_scatter x1, waiting for transfers between devices, on_device(): lax.psum_scatter((summed + jnp.einsum('trc,dc->trd', grad_value_low, w_va...  210 us
    reduce_scatter x1, waiting for transfers between devices, on_device(): lax.psum_scatter(jnp.einsum('nzh,hi->nzi', row_segment, down_weight, pref...  206 us
    reduce_scatter x1, waiting for transfers between devices, on_device(): lax.psum_scatter((jnp.einsum('szq,hq->szh', gate_gradient, gate_weight, p...  191 us
    all_gather x1, waiting for transfers between devices, on_device(): lax.all_gather(grad_middle.astype(jnp.bfloat16), 'head', axis=0, tiled=True)  176 us
    all_gather x1, waiting for transfers between devices, on_device(): lax.all_gather(normed_two_low, 'head', axis=0, tiled=True)  175 us
    all_gather x1, waiting for transfers between devices, on_device(): lax.all_gather(cotangent, 'head', axis=0, tiled=True)  150 us
  transfers between devices with their start and end apart: 23, of which 16 were waited for; matrix products, arithmetic and copies ran while one was open for 12% of the time, Pallas kernels for 0%

profile of v1, /device:TPU:0, one launch (start us, length us, event | category | flops | bytes accessed | tf_op | source)
XLA Modules:
  0.0 2321.1 jit_solution(12737461303045252977)
XLA Ops:
  14.1 37.4 %collective-permute-done = bf16[128,3,2048]{2,0,1:T(8,128)(2,1)S(1)} collective-permute-done((bf16[128,3,2048]{2,0,1:T(8,128)(2,1)S(1)}, bf16[128,3,2048]{2,0,1:T(8,128)(2,1)S(1)}, u32[]{:S(2)}, u32[]{:S(2)}) %collective-permute-start) | collective-permute-done | bytes 1572896 | tf_op jit(solution)/shard_map/ppermute | solution.py:97
  52.6 38.3 %collective-permute-done.1 = bf16[128,3,2048]{2,0,1:T(8,128)(2,1)S(1)} collective-permute-done((bf16[128,3,2048]{2,0,1:T(8,128)(2,1)S(1)}, bf16[128,3,2048]{2,0,1:T(8,128)(2,1)S(1)}, u32[]{:S(2)}, u32[]{:S(2)}) %collective-permute-start.1) | collective-permute-done | bytes 1572896 | tf_op jit(solution)/shard_map/ppermute | solution.py:97
  92.1 37.4 %collective-permute-done.2 = bf16[128,3,2048]{2,0,1:T(8,128)(2,1)S(1)} collective-permute-done((bf16[128,3,2048]{2,0,1:T(8,128)(2,1)S(1)}, bf16[128,3,2048]{2,0,1:T(8,128)(2,1)S(1)}, u32[]{:S(2)}, u32[]{:S(2)}) %collective-permute-start.2) | collective-permute-done | bytes 1572896 | tf_op jit(solution)/shard_map/ppermute | solution.py:97
  130.6 36.4 %collective-permute-done.3 = bf16[128,3,2048]{2,0,1:T(8,128)(2,1)S(1)} collective-permute-done((bf16[128,3,2048]{2,0,1:T(8,128)(2,1)S(1)}, bf16[128,3,2048]{2,0,1:T(8,128)(2,1)S(1)}, u32[]{:S(2)}, u32[]{:S(2)}) %collective-permute-start.3) | collective-permute-done | bytes 1572896 | tf_op jit(solution)/shard_map/ppermute | solution.py:97
  168.2 35.6 %collective-permute-done.4 = bf16[128,3,2048]{2,0,1:T(8,128)(2,1)} collective-permute-done((bf16[128,3,2048]{2,0,1:T(8,128)(2,1)S(1)}, bf16[128,3,2048]{2,0,1:T(8,128)(2,1)}, u32[]{:S(2)}, u32[]{:S(2)}) %collective-permute-start.4) | collective-permute-done | bytes 1572896 | tf_op jit(solution)/shard_map/ppermute | solution.py:97
  203.8 34.9 %collective-permute-done.5 = bf16[128,3,2048]{2,0,1:T(8,128)(2,1)} collective-permute-done((bf16[128,3,2048]{2,0,1:T(8,128)(2,1)}, bf16[128,3,2048]{2,0,1:T(8,128)(2,1)}, u32[]{:S(2)}, u32[]{:S(2)}) %collective-permute-start.5) | collective-permute-done | bytes 1572896 | tf_op jit(solution)/shard_map/ppermute | solution.py:97
  240.7 5.8 all-reduce
  251.2 21.4 collective-permute-done.6
  296.4 14.3 fusion.70
  324.5 5.2 all-gather.2
  329.8 16.6 convert_reduce_fusion
  346.4 8.0 fusion.139
  366.7 10.1 fusion.97
  376.9 410.0 %reduce-scatter.12.cloned.1.call-done = f32[128,3,2048]{2,0,1:T(8,128)} async-done(((f32[1024,3,2048]{2,0,1:T(8,128)}), f32[128,3,2048]{2,0,1:T(8,128)}) %reduce-scatter.12.cloned.1.call-update) | async-done | bytes 3145744 | tf_op jit(solution)/shard_map/reduce_scatter | solution.py:160
  793.6 175.1 %all-gather.11.cloned.1.call-done = bf16[1024,3,2048]{2,0,1:T(8,128)(2,1)} async-done(((bf16[128,3,2048]{2,0,1:T(8,128)(2,1)}), bf16[1024,3,2048]{2,0,1:T(8,128)(2,1)}) %all-gather.11.cloned.1.call-update) | async-done | bytes 12582928 | tf_op jit(solution)/shard_map/all_gather | solution.py:181
  968.7 15.2 fusion.45
  983.9 11.3 fusion.49
  995.1 150.2 %all-gather.13.cloned.1.call-done = bf16[1024,3,2048]{2,0,1:T(8,128)(2,1)} async-done(((bf16[128,3,2048]{2,0,1:T(8,128)(2,1)}), bf16[1024,3,2048]{2,0,1:T(8,128)(2,1)}) %all-gather.13.cloned.1.call-update) | async-done | bytes 12582928 | tf_op jit(solution)/shard_map/all_gather | solution.py:196
  1145.4 22.1 multiply_convert_fusion
  1167.5 17.4 fusion.47
  1184.9 18.9 add_convert_fusion.1
  1203.8 15.0 convolution_convert_fusion
  1219.0 190.8 %reduce-scatter.16.cloned.1.call-done = bf16[128,3,2048]{2,0,1:T(8,128)(2,1)} async-done(((bf16[1024,3,2048]{2,0,1:T(8,128)(2,1)}), bf16[128,3,2048]{2,0,1:T(8,128)(2,1)}) %reduce-scatter.16.cloned.1.call-update) | async-done | bytes 1572880 | tf_op jit(solution)/shard_map/reduce_scatter | solution.py:219
  1413.8 206.4 %reduce-scatter.14.cloned.1.call-done = bf16[128,3,2048]{2,0,1:T(8,128)(2,1)} async-done(((bf16[1024,3,2048]{2,0,1:T(8,128)(2,1)}), bf16[128,3,2048]{2,0,1:T(8,128)(2,1)}) %reduce-scatter.14.cloned.1.call-update) | async-done | bytes 1572880 | tf_op jit(solution)/shard_map/reduce_scatter | solution.py:185
  1620.2 6.0 fusion.135
  1629.2 175.7 %all-gather.15.cloned.1.call-done = bf16[1024,3,2048]{2,0,1:T(8,128)(2,1)} async-done(((bf16[128,3,2048]{2,0,1:T(8,128)(2,1)}), bf16[1024,3,2048]{2,0,1:T(8,128)(2,1)}) %all-gather.15.cloned.1.call-update) | async-done | bytes 12582928 | tf_op jit(solution)/shard_map/all_gather | solution.py:237
  1804.9 9.0 multiply_reduce_fusion.5
  1818.8 14.4 bitcast_convert_fusion
  1833.3 14.3 bitcast_convert_fusion.1
  1847.7 14.8 bitcast_convert_fusion.2
  1868.3 16.5 select_convert_fusion
  1884.9 7.3 fusion.87
  1892.2 8.0 fusion.64
  1900.2 10.2 fusion.114
  1910.4 10.6 fusion.140
  1921.2 10.8 fusion.54
  1932.0 4.9 fusion.124
  1936.9 5.2 all-gather.4
  1942.3 4.9 while.31
  1954.4 8.1 fusion.88
  1964.4 7.5 fusion.67
  1971.9 11.5 fusion.99
  1983.6 8.0 fusion.55
  1991.7 22.2 add_convert_fusion
  2026.5 26.5 %reduce-scatter.24.cloned.1.call-done = bf16[512,256]{1,0:T(8,128)(2,1)} async-done(((bf16[2048,256]{1,0:T(8,128)(2,1)}), bf16[512,256]{1,0:T(8,128)(2,1)}) %reduce-scatter.24.cloned.1.call-update) | async-done | bytes 262160 | tf_op jit(solution)/shard_map/reduce_scatter | solution.py:347
  2054.8 209.9 %reduce-scatter.18.cloned.1.call-done = bf16[128,3,2048]{2,0,1:T(8,128)(2,1)} async-done(((bf16[1024,3,2048]{2,0,1:T(8,128)(2,1)}), bf16[128,3,2048]{2,0,1:T(8,128)(2,1)}) %reduce-scatter.18.cloned.1.call-update) | async-done | bytes 1572880 | tf_op jit(solution)/shard_map/reduce_scatter | solution.py:316
  2267.8 39.7 %all-reduce.4 = (f32[2048]{0:T(1024)S(1)}, f32[2048]{0:T(1024)S(1)}, f32[2048]{0:T(1024)S(1)}) all-reduce(f32[2048]{0:T(1024)S(1)} %get-tuple-element.232, f32[2048]{0:T(1024)S(1)} %copy-done.68, f32[2048]{0:T(1024)S(1)} %copy-done.67), channel_id=11, replica_groups=mesh['seq'=4,'head'=8] {'seq','head'}, use_global_device_ids=true, to_apply=%region_23.24.clone | all-reduce | flops 6144 | bytes 49152
  2309.2 4.9 fusion.28
  (298 shorter events, 125.4 us)
Async XLA Ops:
  7.2 1138.2 %copy-start = (bf16[688,2048]{1,0:T(8,128)(2,1)S(1)}, bf16[688,2048]{1,0:T(8,128)(2,1)}, u32[]{:S(2)}) copy-start(bf16[688,2048]{1,0:T(8,128)(2,1)} %param.27) | copy-start | bytes 8454148
  7.2 231.5 %copy-start.78 = (u32[32]{0:T(128)S(1)}, u32[32]{0:T(128)}, u32[]{:S(2)}) copy-start(u32[32]{0:T(128)} %constant.139) | copy-start | bytes 388
  7.2 232.7 %copy-start.70 = (s32[3,8]{1,0:T(4,128)S(1)}, s32[3,8]{1,0:T(4,128)}, u32[]{:S(2)}) copy-start(s32[3,8]{1,0:T(4,128)} %param.29) | copy-start | bytes 292
  7.2 347.2 %all-gather.17.cloned.1.call-start = ((), (), s32[]{:S(2)}) async-start(), calls=%async_computation.25 | async-start | bytes 2096640 | tf_op jit(solution)/shard_map/all_gather | solution.py:17
  9.2 276.0 %copy-start.65 = (f32[128,3]{0,1:T(4,128)}, f32[128,3]{0,1:T(4,128)S(1)}, u32[]{:S(2)}) copy-start(f32[128,3]{0,1:T(4,128)S(1)} %add_rsqrt_fusion.1) | copy-start | bytes 4612
  11.1 40.4 %collective-permute-start = (bf16[128,3,2048]{2,0,1:T(8,128)(2,1)S(1)}, bf16[128,3,2048]{2,0,1:T(8,128)(2,1)S(1)}, u32[]{:S(2)}, u32[]{:S(2)}) collective-permute-start(bf16[128,3,2048]{2,0,1:T(8,128)(2,1)S(1)} %fusion.33), channel_id=1, source_target_pairs={{0,1},{1,2},{2,3},{3,4},{4,5},{5,6},{6,7},{7,0},{8,9},{9,10},{10,1... | collective-permute-start | bytes 4718600 | tf_op jit(solution)/shard_map/ppermute | solution.py:97
  52.6 38.3 %collective-permute-start.1 = (bf16[128,3,2048]{2,0,1:T(8,128)(2,1)S(1)}, bf16[128,3,2048]{2,0,1:T(8,128)(2,1)S(1)}, u32[]{:S(2)}, u32[]{:S(2)}) collective-permute-start(bf16[128,3,2048]{2,0,1:T(8,128)(2,1)S(1)} %collective-permute-done), channel_id=1, source_target_pairs={{0,1},{1,2},{2,3},{3,4},{4,5},{5,6},{6,7},{7,0},{8,9},{9,10},{10,1... | collective-permute-start | bytes 4718600 | tf_op jit(solution)/shard_map/ppermute | solution.py:97
  92.1 37.4 %collective-permute-start.2 = (bf16[128,3,2048]{2,0,1:T(8,128)(2,1)S(1)}, bf16[128,3,2048]{2,0,1:T(8,128)(2,1)S(1)}, u32[]{:S(2)}, u32[]{:S(2)}) collective-permute-start(bf16[128,3,2048]{2,0,1:T(8,128)(2,1)S(1)} %collective-permute-done.1), channel_id=1, source_target_pairs={{0,1},{1,2},{2,3},{3,4},{4,5},{5,6},{6,7},{7,0},{8,9},{9,10},{10,1... | collective-permute-start | bytes 4718600 | tf_op jit(solution)/shard_map/ppermute | solution.py:97
  130.6 36.4 %collective-permute-start.3 = (bf16[128,3,2048]{2,0,1:T(8,128)(2,1)S(1)}, bf16[128,3,2048]{2,0,1:T(8,128)(2,1)S(1)}, u32[]{:S(2)}, u32[]{:S(2)}) collective-permute-start(bf16[128,3,2048]{2,0,1:T(8,128)(2,1)S(1)} %collective-permute-done.2), channel_id=1, source_target_pairs={{0,1},{1,2},{2,3},{3,4},{4,5},{5,6},{6,7},{7,0},{8,9},{9,10},{10,1... | collective-permute-start | bytes 4718600 | tf_op jit(solution)/shard_map/ppermute | solution.py:97
  168.2 35.6 %collective-permute-start.4 = (bf16[128,3,2048]{2,0,1:T(8,128)(2,1)S(1)}, bf16[128,3,2048]{2,0,1:T(8,128)(2,1)}, u32[]{:S(2)}, u32[]{:S(2)}) collective-permute-start(bf16[128,3,2048]{2,0,1:T(8,128)(2,1)S(1)} %collective-permute-done.3), channel_id=1, source_target_pairs={{0,1},{1,2},{2,3},{3,4},{4,5},{5,6},{6,7},{7,0},{8,9},{9,10},{10,1... | collective-permute-start | bytes 4718600 | tf_op jit(solution)/shard_map/ppermute | solution.py:97
  203.8 34.9 %collective-permute-start.5 = (bf16[128,3,2048]{2,0,1:T(8,128)(2,1)}, bf16[128,3,2048]{2,0,1:T(8,128)(2,1)}, u32[]{:S(2)}, u32[]{:S(2)}) collective-permute-start(bf16[128,3,2048]{2,0,1:T(8,128)(2,1)} %collective-permute-done.4), channel_id=1, source_target_pairs={{0,1},{1,2},{2,3},{3,4},{4,5},{5,6},{6,7},{7,0},{8,9},{9,10},{10,1... | collective-permute-start | bytes 4718600 | tf_op jit(solution)/shard_map/ppermute | solution.py:97
  238.7 34.0 %collective-permute-start.6 = (bf16[128,3,2048]{2,0,1:T(8,128)(2,1)}, bf16[128,3,2048]{2,0,1:T(8,128)(2,1)}, u32[]{:S(2)}, u32[]{:S(2)}) collective-permute-start(bf16[128,3,2048]{2,0,1:T(8,128)(2,1)} %collective-permute-done.5), channel_id=1, source_target_pairs={{0,1},{1,2},{2,3},{3,4},{4,5},{5,6},{6,7},{7,0},{8,9},{9,10},{10,1... | collective-permute-start | bytes 4718600 | tf_op jit(solution)/shard_map/ppermute | solution.py:97
  246.6 114.3 %copy-start.72 = (bf16[273]{0:T(512)(128)(2,1)}, bf16[273]{0:T(512)(128)(2,1)S(1)}, u32[]{:S(2)}) copy-start(bf16[273]{0:T(512)(128)(2,1)S(1)} %pad.3.clone) | copy-start | bytes 1642
  247.7 73.1 %copy-start.52 = (f32[1024,3]{0,1:T(4,128)}, f32[1024,3]{0,1:T(4,128)S(1)}, u32[]{:S(2)}) copy-start(f32[1024,3]{0,1:T(4,128)S(1)} %get-tuple-element.297) | copy-start | bytes 36868
  247.7 113.2 %copy-start.41 = (f32[3,1024]{1,0:T(4,128)}, f32[3,1024]{1,0:T(4,128)S(1)}, u32[]{:S(2)}) copy-start(f32[3,1024]{1,0:T(4,128)S(1)} %get-tuple-element.276) | copy-start | bytes 36868
  251.2 26.4 %copy-start.25 = (bf16[128,3,2048]{2,0,1:T(8,128)(2,1)S(1)}, bf16[128,3,2048]{2,0,1:T(8,128)(2,1)}, u32[]{:S(2)}) copy-start(bf16[128,3,2048]{2,0,1:T(8,128)(2,1)} %copy-done.24) | copy-start | bytes 4718596
  289.8 40.0 %copy-start.31 = (bf16[1024,3,32]{0,2,1:T(8,128)(2,1)}, bf16[1024,3,32]{0,2,1:T(8,128)(2,1)S(1)}, u32[]{:S(2)}) copy-start(bf16[1024,3,32]{0,2,1:T(8,128)(2,1)S(1)} %fusion.89) | copy-start | bytes 589828
  294.7 16.0 copy-start.33
  295.4 21.7 copy-start.15
  320.7 466.2 %reduce-scatter.12.cloned.1.call-start = ((), (), s32[]{:S(2)}) async-start(), calls=%async_computation.11 | async-start | bytes 28311552 | tf_op jit(solution)/shard_map/reduce_scatter | solution.py:160
  329.8 16.6 copy-start.8
  376.8 410.1 %copy-start.69 = (f32[2048]{0:T(1024)S(1)}, f32[2048]{0:T(1024)}, u32[]{:S(2)}) copy-start(f32[2048]{0:T(1024)} %param.23) | copy-start | bytes 24580
  376.8 414.7 %copy-start.64 = (f32[2048]{0:T(1024)S(1)}, f32[2048]{0:T(1024)}, u32[]{:S(2)}) copy-start(f32[2048]{0:T(1024)} %param.24) | copy-start | bytes 24580
  376.9 591.8 %all-gather.11.cloned.1.call-start = ((), (), s32[]{:S(2)}) async-start(), calls=%async_computation.12 | async-start | bytes 14155776 | tf_op jit(solution)/shard_map/all_gather | solution.py:181
  793.0 352.4 %all-gather.13.cloned.1.call-start = ((), (), s32[]{:S(2)}) async-start(), calls=%async_computation.14 | async-start | bytes 14155776 | tf_op jit(solution)/shard_map/all_gather | solution.py:196
  793.6 616.2 %reduce-scatter.16.cloned.1.call-start = ((), (), s32[]{:S(2)}) async-start(), calls=%async_computation.15 | async-start | bytes 14155776 | tf_op jit(solution)/shard_map/reduce_scatter | solution.py:219
  968.7 15.2 copy-start.74
  968.7 15.2 copy-start.75
  1203.8 416.4 %reduce-scatter.14.cloned.1.call-start = ((), (), s32[]{:S(2)}) async-start(), calls=%async_computation.13 | async-start | bytes 14155776 | tf_op jit(solution)/shard_map/reduce_scatter | solution.py:185
  1218.9 401.3 %copy-start.26 = (bf16[128,3,2048]{2,0,1:T(8,128)(2,1)S(1)}, bf16[128,3,2048]{2,0,1:T(8,128)(2,1)}, u32[]{:S(2)}) copy-start(bf16[128,3,2048]{2,0,1:T(8,128)(2,1)} %param.28) | copy-start | bytes 4718596
  1218.9 586.0 %all-gather.15.cloned.1.call-start = ((), (), s32[]{:S(2)}) async-start(), calls=%async_computation.16 | async-start | bytes 14155776 | tf_op jit(solution)/shard_map/all_gather | solution.py:237
  1626.2 178.7 %copy-start.39 = (bf16[256,2048]{1,0:T(8,128)(2,1)S(1)}, bf16[256,2048]{1,0:T(8,128)(2,1)}, u32[]{:S(2)}) copy-start(bf16[256,2048]{1,0:T(8,128)(2,1)} %param.22) | copy-start | bytes 3145732
  1629.2 313.0 %all-gather.19.cloned.1.call-start = ((), (), s32[]{:S(2)}) async-start(), calls=%async_computation.26 | async-start | bytes 2096640 | tf_op jit(solution)/shard_map/all_gather | solution.py:17
  1814.4 48.3 %copy-start.10 = (bf16[1024,3,2,128]{0,3,2,1:T(8,128)(2,1)}, bf16[1024,3,2,128]{0,3,2,1:T(8,128)(2,1)S(1)}, u32[]{:S(2)}) copy-start(bf16[1024,3,2,128]{0,3,2,1:T(8,128)(2,1)S(1)} %divide_convert_fusion) | copy-start | bytes 4718596
  1818.8 195.2 %reduce-scatter.32.cloned.1.call-start = ((), (), s32[]{:S(2)}) async-start(), calls=%async_computation.24 | async-start | bytes 3522560 | tf_op jit(solution)/shard_map/reduce_scatter | solution.py:359
  1833.3 183.1 %reduce-scatter.30.cloned.1.call-start = ((), (), s32[]{:S(2)}) async-start(), calls=%async_computation.23 | async-start | bytes 3522560 | tf_op jit(solution)/shard_map/reduce_scatter | solution.py:356
  1847.6 171.2 %reduce-scatter.28.cloned.1.call-start = ((), (), s32[]{:S(2)}) async-start(), calls=%async_computation.22 | async-start | bytes 3522560 | tf_op jit(solution)/shard_map/reduce_scatter | solution.py:353
  1862.5 158.7 %reduce-scatter.20.cloned.1.call-start = ((), (), s32[]{:S(2)}) async-start(), calls=%async_computation.18 | async-start | bytes 163840 | tf_op jit(solution)/shard_map/reduce_scatter | solution.py:341
  1868.3 16.5 copy-start.35
  1921.0 101.6 %reduce-scatter.26.cloned.1.call-start = ((), (), s32[]{:S(2)}) async-start(), calls=%async_computation.21 | async-start | bytes 1310720 | tf_op jit(solution)/shard_map/reduce_scatter | solution.py:350
  1942.1 83.0 %reduce-scatter.22.cloned.1.call-start = ((), (), s32[]{:S(2)}) async-start(), calls=%async_computation.19 | async-start | bytes 163840 | tf_op jit(solution)/shard_map/reduce_scatter | solution.py:344
  1983.4 69.6 %reduce-scatter.24.cloned.1.call-start = ((), (), s32[]{:S(2)}) async-start(), calls=%async_computation.20 | async-start | bytes 1310720 | tf_op jit(solution)/shard_map/reduce_scatter | solution.py:347
  1991.6 273.0 %reduce-scatter.18.cloned.1.call-start = ((), (), s32[]{:S(2)}) async-start(), calls=%async_computation.17 | async-start | bytes 14155776 | tf_op jit(solution)/shard_map/reduce_scatter | solution.py:316
  2014.0 250.7 %copy-start.57 = (f32[2048]{0:T(1024)S(1)}, f32[2048]{0:T(1024)}, u32[]{:S(2)}) copy-start(f32[2048]{0:T(1024)} %param.18) | copy-start | bytes 24580
  2014.0 250.7 %copy-start.66 = (f32[128,3]{0,1:T(4,128)S(1)}, f32[128,3]{0,1:T(4,128)}, u32[]{:S(2)}) copy-start(f32[128,3]{0,1:T(4,128)} %copy-done.65) | copy-start | bytes 4612
  2016.4 251.4 %copy-start.67 = (f32[2048]{0:T(1024)S(1)}, f32[2048]{0:T(1024)}, u32[]{:S(2)}) copy-start(f32[2048]{0:T(1024)} %get-tuple-element.230) | copy-start | bytes 24580
  2016.4 251.4 %copy-start.68 = (f32[2048]{0:T(1024)S(1)}, f32[2048]{0:T(1024)}, u32[]{:S(2)}) copy-start(f32[2048]{0:T(1024)} %get-tuple-element.271) | copy-start | bytes 24580
  2264.6 49.6 %copy-start.1 = (bf16[688,2048]{1,0:T(8,128)(2,1)S(1)}, bf16[688,2048]{1,0:T(8,128)(2,1)}, u32[]{:S(2)}) copy-start(bf16[688,2048]{1,0:T(8,128)(2,1)} %param.27) | copy-start | bytes 8454148
  (54 other events, 301.3 us)
Sparse Core Ops, SparseCore 0:
  320.9 16.2 all-gather.16
  377.0 409.9 reduce-scatter.11
  793.1 175.5 all-gather.10
  970.7 174.6 all-gather.12
  1203.9 205.8 reduce-scatter.15
  1413.2 206.8 reduce-scatter.13
  1629.3 175.5 all-gather.14
  1818.9 18.4 all-gather.18
  1840.0 35.8 reduce-scatter.31
  1878.5 35.8 reduce-scatter.29
  1917.0 36.0 reduce-scatter.27
  1956.1 19.5 reduce-scatter.19
  1978.2 24.8 reduce-scatter.25
  2005.5 19.5 reduce-scatter.21
  2028.1 24.8 reduce-scatter.23
  2056.9 207.7 reduce-scatter.17
